TPU v7x, 256 devices: a whole 4x4x8 slice. The times are simulated.
256 devices in a mesh: gx: 16 (over x, y), gy: 2 (over core), gz: 8 (over z).
Axes of the slice: x: 4, y: 4, z: 8, core: 2. Of those that a mesh axis runs over, the one named last changes fastest.
Arguments:
- field: float32 [2, 1024, 128, 1024], P(None, 'gx', 'gy', 'gz'), as said below
- start_basis: float32 [1024, 256], replicated, may hold values from -6 to 6
Outputs:
- factor: float32 [1024, 256], P('gx')
- core: float32 [2, 256, 128, 1024], P(None, 'gx', 'gy', 'gz')
Inputs may be any that keep to these rules, and one draw needn't show every extreme that they name: Real-valued field; no structure is promised.
All inputs are finite; a program needn't handle non-finite values.
Results may differ from a plain program's by a relative error of at most 0.0002.
Values sent between devices are 32-bit elements; how exact they have to be, the bound alone decides.
A program may use at most 64 MiB of HBM per device.

v0:
```python
import jax
import jax.numpy as jnp
from jax import lax
from jax.sharding import PartitionSpec as P

ITERS = 2


def orthonormal(image):
    small = jnp.dot(image.T, image, precision=lax.Precision.HIGHEST)
    lower = jnp.linalg.cholesky(small)
    return jax.scipy.linalg.solve_triangular(lower, image.T, lower=True).T


def per_device(field, start_basis):
    comps, slab, cells_y, cells_z = field.shape
    flat_field = field.reshape(comps, slab, cells_y * cells_z)
    fibers = lax.all_to_all(flat_field, "gx", split_axis=2, concat_axis=1, tiled=True)
    basis = start_basis
    local_gram = jnp.einsum("crm,csm->rs", fibers, fibers, precision=lax.Precision.HIGHEST)
    gram = lax.psum(local_gram, ("gx", "gy", "gz"))
    for step in range(ITERS):
        image = jnp.dot(gram, basis, precision=lax.Precision.HIGHEST)
        basis = orthonormal(image)
    projected = jnp.einsum("rk,crm->ckm", basis, fibers, precision=lax.Precision.HIGHEST)
    returned = lax.all_to_all(projected, "gx", split_axis=1, concat_axis=2, tiled=True)
    offset = lax.axis_index("gx") * slab
    factor = lax.dynamic_slice_in_dim(basis, offset, slab, 0)
    return (factor, returned.reshape(comps, returned.shape[1], cells_y, cells_z))


def solution(mesh):
    placed = (P(None, "gx", "gy", "gz"), P())
    return jax.shard_map(
        per_device,
        mesh=mesh,
        in_specs=placed,
        out_specs=(P("gx", None), P(None, "gx", "gy", "gz")),
        check_vma=False,
    )
```

profile of v0, /device:TPU:97, one launch (start us, length us, event | category | flops | bytes accessed | tf_op | source)
XLA Modules:
  0.0 604.0 jit_solution(12621777568615691695)
XLA Ops:
  7.2 8.4 %copy.13 = f32[2,64,64,128]{1,0,3,2:T(2,128)} copy(f32[2,64,64,128]{3,2,1,0:T(8,128)} %param.5) | data formatting | bytes 8388608 | tf_op args[0]
  15.7 15.1 %reshape.52 = f32[16,1,65536]{2,1,0:T(1,128)} reshape(f32[8192,2,64]{2,1,0:T(2,128)} %bitcast.97) | data formatting | bytes 8388608
  30.8 56.1 %all_to_all.33 = f32[16,1,65536]{2,1,0:T(1,128)} all-to-all(f32[16,1,65536]{2,1,0:T(1,128)} %reshape.52), channel_id=1, replica_groups=mesh['gx'=16,'gy'=2,'gz'=8] {'gx'}, dimensions={0} | all-to-all | bytes 8388608 | tf_op jit(solution)/shard_map/all_to_all | solution.py:18
  87.3 13.7 %reduce.8 = f32[16,65536]{1,0:T(8,128)} reduce(f32[16,1,65536]{2,1,0:T(1,128)} %all_to_all.33, f32[]{:T(128)} %broadcast.87), dimensions={1}, to_apply=%all_to_all.24.reduce_sub_computation | reduce | bytes 8388612 | tf_op jit(solution)/shard_map/all_to_all | solution.py:18
  101.0 9.7 %reshape.53 = f32[8192,2,64]{2,1,0:T(2,128)} reshape(f32[16,65536]{1,0:T(8,128)} %reduce.8) | data formatting | bytes 8388608
  110.7 12.2 %copy.26 = f32[2,64,16,512]{3,1,2,0:T(8,128)} copy(f32[2,64,16,512]{1,0,3,2:T(2,128)} %bitcast.96) | data formatting | bytes 8388608 | tf_op jit(solution)/shard_map/all_to_all | solution.py:18
  122.9 17.6 %convolution_bitcast_fusion = f32[1024,1024]{1,0:T(8,128)} fusion(f32[2,1024,512]{2,1,0:T(8,128)} %bitcast.98), kind=kOutput, calls=%fused_computation.4 | convolution fusion | flops 12884901888 | bytes 8388608 | tf_op jit(solution)/shard_map/crm,csm->rs/dot_general | solution.py:20
  140.6 270.4 %all-reduce.3.cloned.1.call-done = f32[1024,1024]{1,0:T(8,128)} async-done(((f32[1024,1024]{1,0:T(8,128)}), f32[1024,1024]{1,0:T(8,128)}) %all-reduce.3.cloned.1.call-update) | async-done | bytes 4194320 | tf_op jit(solution)/shard_map/psum | solution.py:21
  411.0 5.5 fusion.32
  416.5 1.8 fusion.33
  418.5 11.7 %cholesky.130 = f32[128,128]{1,0:T(8,128)S(1)} custom-call(f32[128,128]{1,0:T(8,128)S(1)} %cholesky.194), custom_call_target="Cholesky" | custom-call | tf_op jit(solution)/shard_map/jit(cholesky)/cholesky | solution.py:11
  430.3 9.8 %custom-call.13 = f32[1,128,128]{1,2,0:T(8,128)S(1)} custom-call(f32[1,128,128]{2,1,0:T(8,128)S(1)} %get-tuple-element.53), custom_call_target="InvertDiagBlocksLowerTriangular" | custom-call | tf_op jit(solution)/shard_map/jit(cholesky)/cholesky | solution.py:11
  440.6 11.7 %cholesky.147 = f32[128,128]{1,0:T(8,128)S(1)} custom-call(f32[128,128]{1,0:T(8,128)S(1)} %convolution_subtract_fusion.3), custom_call_target="Cholesky" | custom-call | tf_op jit(solution)/shard_map/jit(cholesky)/cholesky | solution.py:11
  467.2 3.9 while.4
  471.2 19.7 %custom-call.14 = f32[2,128,128]{1,2,0:T(8,128)S(1)} custom-call(f32[2,128,128]{2,1,0:T(8,128)S(1)} %get-tuple-element.18), custom_call_target="InvertDiagBlocksLowerTriangular" | custom-call | tf_op jit(solution)/shard_map/jit(_solve_triangular)/triangular_solve | solution.py:12
  493.2 5.3 fusion.2
  500.5 11.7 %cholesky.164 = f32[128,128]{1,0:T(8,128)S(1)} custom-call(f32[128,128]{1,0:T(8,128)S(1)} %cholesky.197), custom_call_target="Cholesky" | custom-call | tf_op jit(solution)/shard_map/jit(cholesky)/cholesky | solution.py:11
  512.3 9.8 %custom-call.15 = f32[1,128,128]{1,2,0:T(8,128)S(1)} custom-call(f32[1,128,128]{2,1,0:T(8,128)S(1)} %get-tuple-element.49), custom_call_target="InvertDiagBlocksLowerTriangular" | custom-call | tf_op jit(solution)/shard_map/jit(cholesky)/cholesky | solution.py:11
  522.6 11.7 %cholesky.181 = f32[128,128]{1,0:T(8,128)S(1)} custom-call(f32[128,128]{1,0:T(8,128)S(1)} %convolution_subtract_fusion.2), custom_call_target="Cholesky" | custom-call | tf_op jit(solution)/shard_map/jit(cholesky)/cholesky | solution.py:11
  537.2 4.0 while.5
  541.2 19.7 %custom-call.16 = f32[2,128,128]{1,2,0:T(8,128)S(1)} custom-call(f32[2,128,128]{2,1,0:T(8,128)S(1)} %get-tuple-element.19), custom_call_target="InvertDiagBlocksLowerTriangular" | custom-call | tf_op jit(solution)/shard_map/jit(_solve_triangular)/triangular_solve | solution.py:12
  563.2 5.7 convolution_bitcast_fusion.1
  570.7 4.6 all-to-all-start.1
  576.1 17.8 %all-to-all-done.1 = f32[2,256,512]{2,0,1:T(2,128)} async-done(((f32[2,256,512]{2,0,1:T(2,128)}), f32[2,256,512]{2,0,1:T(2,128)}, u32[]{:S(2)}, u32[]{:S(2)}) %all-to-all-start.1) | async-done | bytes 1048608 | tf_op jit(solution)/shard_map/all_to_all | solution.py:26
  (54 shorter events, 24.0 us)
Async XLA Ops:
  7.2 403.9 %copy-start = (f32[1024,256]{1,0:T(8,128)S(1)}, f32[1024,256]{1,0:T(8,128)}, u32[]{:S(2)}) copy-start(f32[1024,256]{1,0:T(8,128)} %param.6) | copy-start | bytes 3145732
  7.2 403.8 %all-reduce.3.cloned.1.call-start = ((), (), s32[]{:S(2)}) async-start(), calls=%async_computation.2 | async-start | bytes 8388608 | tf_op jit(solution)/shard_map/psum | solution.py:21
  570.7 23.2 %all-to-all-start.1 = ((f32[2,256,512]{2,0,1:T(2,128)}), f32[2,256,512]{2,0,1:T(2,128)}, u32[]{:S(2)}, u32[]{:S(2)}) async-start(f32[2,256,512]{2,0,1:T(2,128)} %copy.20), calls=%async_computation.1 | async-start | bytes 2097152 | tf_op jit(solution)/shard_map/all_to_all | solution.py:26
Sparse Core Ops, SparseCore 0:
  140.7 270.2 all-reduce.2
where the time goes:
time: 614 us; the launch traced here: 604 us
  waiting for transfers between devices  288 us (47%)
  other arithmetic  122 us (20%)
  local copies, waits for them, and re-layouts  59.5 us (10%)
  blocking collectives  56.1 us (9%)
  matrix products  43.3 us (7%)
  between operations  30.1 us (5%)
    psum x1, waiting for transfers between devices, per_device(): gram = lax.psum(local_gram, ('gx', 'gy', 'gz'))  270 us
    another operation x13, other arithmetic, orthonormal(): lower = jnp.linalg.cholesky(small)  68.5 us
    all_to_all x1, blocking collectives, per_device(): lax.all_to_all(flat_field, 'gx', split_axis=2, concat_axis=1, tiled=True)  56.1 us
    another operation x5, other arithmetic, orthonormal(): return jax.scipy.linalg.solve_triangular(lower, image.T, lower=True).T  39.6 us
    unnamed x6, local copies, waits for them, and re-layouts  33.9 us
    all_to_all x1, waiting for transfers between devices, per_device(): lax.all_to_all(projected, 'gx', split_axis=1, concat_axis=2, tiled=True)  17.8 us
    dot_general x1, matrix products, per_device(): jnp.einsum('crm,csm->rs', fibers, fibers, precision=lax.Precision.HIGHEST)  17.6 us
    all_to_all x1, other arithmetic, per_device(): lax.all_to_all(flat_field, 'gx', split_axis=2, concat_axis=1, tiled=True)  13.7 us
  transfers between devices with their start and end apart: 2, of which 2 were waited for; matrix products, arithmetic and copies ran while one was open for 0% of the time, Pallas kernels for 0%

commit v1 on v0

--- a/solution.py
+++ b/solution.py
@@ -18,7 +18,9 @@
     fibers = lax.all_to_all(flat_field, "gx", split_axis=2, concat_axis=1, tiled=True)
     basis = start_basis
     local_gram = jnp.einsum("crm,csm->rs", fibers, fibers, precision=lax.Precision.HIGHEST)
-    gram = lax.psum(local_gram, ("gx", "gy", "gz"))
+    gram = local_gram
+    for name in (("gy", "gz"), "gx"):
+        gram = lax.psum(gram, name)
     for step in range(ITERS):
         image = jnp.dot(gram, basis, precision=lax.Precision.HIGHEST)
         basis = orthonormal(image)

time: 614 us -> 584 us (0.951)
  the two profiles are of different devices: /device:TPU:97 before, /device:TPU:32 now
where the time goes in v1:
time: 584 us; the launch traced here: 573 us
  waiting for transfers between devices  255 us (44%)
  other arithmetic  122 us (21%)
  local copies, waits for them, and re-layouts  59.5 us (10%)
  blocking collectives  57.9 us (10%)
  matrix products  43 us (7%)
  between operations  30.1 us (5%)
    psum x2, waiting for transfers between devices, per_device(): gram = lax.psum(gram, name)  238 us
    another operation x13, other arithmetic, orthonormal(): lower = jnp.linalg.cholesky(small)  68.5 us
    all_to_all x1, blocking collectives, per_device(): lax.all_to_all(flat_field, 'gx', split_axis=2, concat_axis=1, tiled=True)  57.9 us
    another operation x5, other arithmetic, orthonormal(): return jax.scipy.linalg.solve_triangular(lower, image.T, lower=True).T  39.6 us
    unnamed x6, local copies, waits for them, and re-layouts  33.9 us
    dot_general x1, matrix products, per_device(): jnp.einsum('crm,csm->rs', fibers, fibers, precision=lax.Precision.HIGHEST)  17.6 us
    all_to_all x1, waiting for transfers between devices, per_device(): lax.all_to_all(projected, 'gx', split_axis=1, concat_axis=2, tiled=True)  16.9 us
    all_to_all x1, other arithmetic, per_device(): lax.all_to_all(flat_field, 'gx', split_axis=2, concat_axis=1, tiled=True)  13.7 us
  transfers between devices with their start and end apart: 3, of which 3 were waited for; matrix products, arithmetic and copies ran while one was open for 0% of the time, Pallas kernels for 0%

profile of v1, /device:TPU:32, one launch (start us, length us, event | category | flops | bytes accessed | tf_op | source)
XLA Modules:
  0.0 573.4 jit_solution(10186639585746647599)
XLA Ops:
  7.2 8.4 %copy.13 = f32[2,64,64,128]{1,0,3,2:T(2,128)} copy(f32[2,64,64,128]{3,2,1,0:T(8,128)} %param.5) | data formatting | bytes 8388608 | tf_op args[0]
  15.7 15.1 %reshape.52 = f32[16,1,65536]{2,1,0:T(1,128)} reshape(f32[8192,2,64]{2,1,0:T(2,128)} %bitcast.97) | data formatting | bytes 8388608
  30.8 57.9 %all_to_all.33 = f32[16,1,65536]{2,1,0:T(1,128)} all-to-all(f32[16,1,65536]{2,1,0:T(1,128)} %reshape.52), channel_id=1, replica_groups=mesh['gx'=16,'gy'=2,'gz'=8] {'gx'}, dimensions={0} | all-to-all | bytes 8388608 | tf_op jit(solution)/shard_map/all_to_all | solution.py:18
  89.1 13.7 %reduce.8 = f32[16,65536]{1,0:T(8,128)} reduce(f32[16,1,65536]{2,1,0:T(1,128)} %all_to_all.33, f32[]{:T(128)} %broadcast.87), dimensions={1}, to_apply=%all_to_all.24.reduce_sub_computation | reduce | bytes 8388612 | tf_op jit(solution)/shard_map/all_to_all | solution.py:18
  102.9 9.7 %reshape.53 = f32[8192,2,64]{2,1,0:T(2,128)} reshape(f32[16,65536]{1,0:T(8,128)} %reduce.8) | data formatting | bytes 8388608
  112.5 12.2 %copy.26 = f32[2,64,16,512]{3,1,2,0:T(8,128)} copy(f32[2,64,16,512]{1,0,3,2:T(2,128)} %bitcast.96) | data formatting | bytes 8388608 | tf_op jit(solution)/shard_map/all_to_all | solution.py:18
  124.7 17.6 %convolution_bitcast_fusion = f32[1024,1024]{1,0:T(8,128)} fusion(f32[2,1024,512]{2,1,0:T(8,128)} %bitcast.98), kind=kOutput, calls=%fused_computation.4 | convolution fusion | flops 12884901888 | bytes 8388608 | tf_op jit(solution)/shard_map/crm,csm->rs/dot_general | solution.py:20
  142.7 118.2 %all-reduce.4.cloned.1.call-done = f32[1024,1024]{1,0:T(8,128)} async-done(((f32[1024,1024]{1,0:T(8,128)}), f32[1024,1024]{1,0:T(8,128)}) %all-reduce.4.cloned.1.call-update) | async-done | bytes 4194320 | tf_op jit(solution)/shard_map/psum | solution.py:23
  260.9 119.8 %all-reduce.6.cloned.1.call-done = f32[1024,1024]{1,0:T(8,128)} async-done(((f32[1024,1024]{1,0:T(8,128)}), f32[1024,1024]{1,0:T(8,128)}) %all-reduce.6.cloned.1.call-update) | async-done | bytes 4194320 | tf_op jit(solution)/shard_map/psum | solution.py:23
  380.7 5.2 fusion.32
  388.0 11.7 %cholesky.130 = f32[128,128]{1,0:T(8,128)S(1)} custom-call(f32[128,128]{1,0:T(8,128)S(1)} %cholesky.194), custom_call_target="Cholesky" | custom-call | tf_op jit(solution)/shard_map/jit(cholesky)/cholesky | solution.py:11
  399.7 9.8 %custom-call.13 = f32[1,128,128]{1,2,0:T(8,128)S(1)} custom-call(f32[1,128,128]{2,1,0:T(8,128)S(1)} %get-tuple-element.53), custom_call_target="InvertDiagBlocksLowerTriangular" | custom-call | tf_op jit(solution)/shard_map/jit(cholesky)/cholesky | solution.py:11
  410.0 11.7 %cholesky.147 = f32[128,128]{1,0:T(8,128)S(1)} custom-call(f32[128,128]{1,0:T(8,128)S(1)} %convolution_subtract_fusion.3), custom_call_target="Cholesky" | custom-call | tf_op jit(solution)/shard_map/jit(cholesky)/cholesky | solution.py:11
  436.7 3.9 while.4
  440.6 19.7 %custom-call.14 = f32[2,128,128]{1,2,0:T(8,128)S(1)} custom-call(f32[2,128,128]{2,1,0:T(8,128)S(1)} %get-tuple-element.18), custom_call_target="InvertDiagBlocksLowerTriangular" | custom-call | tf_op jit(solution)/shard_map/jit(_solve_triangular)/triangular_solve | solution.py:12
  462.6 5.3 fusion.2
  470.0 11.7 %cholesky.164 = f32[128,128]{1,0:T(8,128)S(1)} custom-call(f32[128,128]{1,0:T(8,128)S(1)} %cholesky.197), custom_call_target="Cholesky" | custom-call | tf_op jit(solution)/shard_map/jit(cholesky)/cholesky | solution.py:11
  481.7 9.8 %custom-call.15 = f32[1,128,128]{1,2,0:T(8,128)S(1)} custom-call(f32[1,128,128]{2,1,0:T(8,128)S(1)} %get-tuple-element.49), custom_call_target="InvertDiagBlocksLowerTriangular" | custom-call | tf_op jit(solution)/shard_map/jit(cholesky)/cholesky | solution.py:11
  492.0 11.7 %cholesky.181 = f32[128,128]{1,0:T(8,128)S(1)} custom-call(f32[128,128]{1,0:T(8,128)S(1)} %convolution_subtract_fusion.2), custom_call_target="Cholesky" | custom-call | tf_op jit(solution)/shard_map/jit(cholesky)/cholesky | solution.py:11
  506.6 4.0 while.5
  510.6 19.7 %custom-call.16 = f32[2,128,128]{1,2,0:T(8,128)S(1)} custom-call(f32[2,128,128]{2,1,0:T(8,128)S(1)} %get-tuple-element.19), custom_call_target="InvertDiagBlocksLowerTriangular" | custom-call | tf_op jit(solution)/shard_map/jit(_solve_triangular)/triangular_solve | solution.py:12
  532.6 5.7 convolution_bitcast_fusion.1
  540.1 5.4 all-to-all-start.1
  546.3 16.9 %all-to-all-done.1 = f32[2,256,512]{2,0,1:T(2,128)} async-done(((f32[2,256,512]{2,0,1:T(2,128)}), f32[2,256,512]{2,0,1:T(2,128)}, u32[]{:S(2)}, u32[]{:S(2)}) %all-to-all-start.1) | async-done | bytes 1048608 | tf_op jit(solution)/shard_map/all_to_all | solution.py:28
  (57 shorter events, 26.2 us)
Async XLA Ops:
  7.2 373.5 %copy-start = (f32[1024,256]{1,0:T(8,128)S(1)}, f32[1024,256]{1,0:T(8,128)}, u32[]{:S(2)}) copy-start(f32[1024,256]{1,0:T(8,128)} %param.6) | copy-start | bytes 3145732
  7.2 253.7 %all-reduce.4.cloned.1.call-start = ((), (), s32[]{:S(2)}) async-start(), calls=%async_computation.2 | async-start | bytes 8388608 | tf_op jit(solution)/shard_map/psum | solution.py:23
  142.4 238.3 %all-reduce.6.cloned.1.call-start = ((), (), s32[]{:S(2)}) async-start(), calls=%async_computation.3 | async-start | bytes 8388608 | tf_op jit(solution)/shard_map/psum | solution.py:23
  540.1 23.1 %all-to-all-start.1 = ((f32[2,256,512]{2,0,1:T(2,128)}), f32[2,256,512]{2,0,1:T(2,128)}, u32[]{:S(2)}, u32[]{:S(2)}) async-start(f32[2,256,512]{2,0,1:T(2,128)} %copy.20), calls=%async_computation.1 | async-start | bytes 2097152 | tf_op jit(solution)/shard_map/all_to_all | solution.py:28
Sparse Core Ops, SparseCore 0:
  142.5 118.3 all-reduce.3
  264.2 116.4 all-reduce.5
